TPU v7x, 32 devices: a whole 2x2x4 slice. The times are simulated.
32 devices in a mesh: dp: 2 (over y), expert: 16 (over z, x, core).
Axes of the slice: x: 2, y: 2, z: 4, core: 2. Of those that a mesh axis runs over, the one named last changes fastest.
Arguments:
- soft_tokens: bfloat16 [2048, 2048], P('expert', 'dp'), may hold values from -6 to 6
- expert_ids: int32 [2048, 8], P('expert'), may hold values from 0 to 31, all different within a row; in each aligned block of 128 rows (0 to 127, 128 to 255, ...) at most 40 rows name the same one
- gate_mix: float32 [2048, 8], P('expert'), may hold values from 0.05 to 0.35
- w_gate: bfloat16 [32, 2048, 768], P('expert', 'dp'), may hold values from -0.125 to 0.125
- w_up: bfloat16 [32, 2048, 768], P('expert', 'dp'), may hold values from -0.125 to 0.125
- w_down: bfloat16 [32, 768, 2048], P('expert', None, 'dp'), may hold values from -0.21875 to 0.21875
- out_grad: bfloat16 [2048, 2048], P('expert', 'dp'), may hold values from -6 to 6
Outputs:
- mixed: bfloat16 [2048, 2048], P('expert', 'dp')
- token_grad: bfloat16 [2048, 2048], P('expert', 'dp')
Inputs may be any that keep to these rules, and one draw needn't show every extreme that they name: `expert_ids`: each row names 8 different experts. Among the 128 rows of one device no expert is named by more than 40 rows, and in some device one expert is named by exactly 40 rows.
All inputs are finite; a program needn't handle non-finite values.
Results may differ from a plain program's by a relative error of at most 0.023.
Values may be sent and summed in bfloat16 or wider, within the bound.
A program may use at most 128 MiB of HBM per device.

v0:
```python
import jax
import jax.numpy as jnp
from jax import lax
from jax.sharding import PartitionSpec as P


def slot_table(expert_ids, experts, capacity):
    tok_rows, top_count = expert_ids.shape
    flat_count = tok_rows * top_count
    flat_ids = expert_ids.reshape(flat_count)
    onehot = (flat_ids[:, None] == jnp.arange(experts, dtype=jnp.int32)[None, :]).astype(jnp.int32)
    before = jnp.sum(jnp.cumsum(onehot, axis=0) * onehot, axis=1) - 1
    position = flat_ids * capacity + before
    source = jnp.full((experts * capacity,), flat_count, jnp.int32)
    source = source.at[position].set(jnp.arange(flat_count, dtype=jnp.int32))
    return (position, source)


def place_rows(values, source, top_count):
    tok_rows = values.shape[0]
    valid = source < tok_rows * top_count
    token = jnp.minimum(source // top_count, tok_rows - 1)
    return jnp.where(valid[:, None], values[token], jnp.zeros((), values.dtype))


def activate(sums, hidden):
    gate_part = sums[..., :hidden]
    upper_part = sums[..., hidden:]
    sigmoid_gate = jax.nn.sigmoid(gate_part)
    return (gate_part * sigmoid_gate * upper_part).astype(jnp.bfloat16)


def act_grad(sums, back, hidden):
    gate_part = sums[..., :hidden]
    upper_part = sums[..., hidden:]
    sigmoid_gate = jax.nn.sigmoid(gate_part)
    d_gate = back * upper_part * sigmoid_gate * (1.0 + gate_part * (1.0 - sigmoid_gate))
    d_upper = back * gate_part * sigmoid_gate
    return jnp.concatenate([d_gate, d_upper], axis=-1).astype(jnp.bfloat16)


def combine(returned, position, gate_mix):
    tok_rows, top_count = gate_mix.shape
    flat_rows = returned.reshape(-1, returned.shape[-1])
    picked = flat_rows[position].reshape(tok_rows, top_count, -1).astype(jnp.float32)
    return jnp.sum(gate_mix[:, :, None] * picked, axis=1).astype(jnp.bfloat16)


def per_device(soft_tokens, expert_ids, gate_mix, w_gate, w_up, w_down, out_grad):
    tok_rows, width_part = soft_tokens.shape
    top_count = expert_ids.shape[1]
    local_experts = w_gate.shape[0]
    hidden = w_gate.shape[2]
    groups = lax.axis_size("expert")
    experts = groups * local_experts
    capacity = max(2, tok_rows * top_count * 5 // (4 * experts))
    position, source = slot_table(expert_ids, experts, capacity)
    w_both = jnp.concatenate([w_gate, w_up], axis=2)
    layout = (groups, local_experts, capacity, width_part)
    token_rows = place_rows(soft_tokens, source, top_count).reshape(layout)
    grad_rows_out = place_rows(out_grad, source, top_count).reshape(layout)
    token_recv = lax.all_to_all(token_rows, "expert", split_axis=0, concat_axis=0, tiled=True)
    dp_count = lax.axis_size("dp")
    share = groups // dp_count
    first_row = lax.axis_index("dp") * share
    piece = token_recv
    own_sums = lax.psum_scatter(
        jnp.einsum("secd,edf->secf", piece, w_both, preferred_element_type=jnp.float32).astype(
            jnp.bfloat16
        ),
        "dp",
        scatter_dimension=0,
        tiled=True,
    ).astype(jnp.float32)
    hidden_act = lax.all_gather(activate(own_sums, hidden), "dp", axis=0, tiled=True)
    expert_out = jnp.einsum(
        "secf,efd->secd", hidden_act, w_down, preferred_element_type=jnp.float32
    ).astype(jnp.bfloat16)
    out_returned = lax.all_to_all(expert_out, "expert", split_axis=0, concat_axis=0, tiled=True)
    grad_recv = lax.all_to_all(grad_rows_out, "expert", split_axis=0, concat_axis=0, tiled=True)
    piece = grad_recv
    whole_back = lax.psum(
        jnp.einsum("secd,efd->secf", piece, w_down, preferred_element_type=jnp.float32).astype(
            jnp.bfloat16
        ),
        "dp",
    ).astype(jnp.float32)
    own_back = lax.dynamic_slice_in_dim(whole_back, first_row, share, 0)
    dpre = lax.all_gather(act_grad(own_sums, own_back, hidden), "dp", axis=0, tiled=True)
    grad_rows = jnp.einsum(
        "secf,edf->secd", dpre, w_both, preferred_element_type=jnp.float32
    ).astype(jnp.bfloat16)
    grad_returned = lax.all_to_all(grad_rows, "expert", split_axis=0, concat_axis=0, tiled=True)
    mixed = combine(out_returned, position, gate_mix)
    token_grad = combine(grad_returned, position, gate_mix)
    return (mixed, token_grad)


def solution(mesh):
    in_specs = (
        P("expert", "dp"),
        P("expert", None),
        P("expert", None),
        P("expert", "dp", None),
        P("expert", "dp", None),
        P("expert", None, "dp"),
        P("expert", "dp"),
    )
    out_specs = (P("expert", "dp"), P("expert", "dp"))
    return jax.shard_map(
        per_device, mesh=mesh, in_specs=in_specs, out_specs=out_specs, check_vma=False
    )
```

profile of v0, /device:TPU:11, one launch (start us, length us, event | category | flops | bytes accessed | tf_op | source)
XLA Modules:
  0.0 453.7 jit_solution(9259662578411656731)
XLA Ops:
  7.2 1.0 copy.23
  9.0 1.3 broadcast_multiply_fusion
  10.9 15.7 %reduce-window.6 = s32[32,8,128]{2,1,0:T(8,128)S(1)} reduce-window(s32[32,8,128]{2,1,0:T(8,128)} %fusion.23, s32[]{:T(128)} %constant.19.clone.1), window={size=1x1x128 pad=0_0x0_0x127_0}, to_apply=%region_0.0 | reduce-window | flops 4161536 | bytes 262148 | tf_op jit(solution)/shard_map/reduce-window
  27.4 1.0 copy.25
  31.5 4.3 scatter_custom_fusion
  35.9 5.1 %gather_fusion.2 = bf16[1280,1024]{1,0:T(8,128)(2,1)} fusion(bf16[128,1024]{1,0:T(8,128)(2,1)S(1)} %copy-done.1, s32[2048]{0:T(1024)S(1)} %pad_clamp_fusion), kind=kCustom, calls=%fused_computation.2 | custom fusion | bytes 5248000 | tf_op jit(solution)/shard_map/gather | solution.py:23
  41.0 7.7 %gather_fusion = bf16[1280,1024]{1,0:T(8,128)(2,1)} fusion(bf16[128,1024]{1,0:T(8,128)(2,1)} %param.7, s32[2048]{0:T(1024)S(1)} %pad_clamp_fusion), kind=kCustom, calls=%fused_computation | custom fusion | bytes 5248000 | tf_op jit(solution)/shard_map/gather | solution.py:23
  48.8 3.9 broadcast_select_fusion
  52.7 64.9 %all_to_all.20 = bf16[16,2,40,1024]{3,2,1,0:T(8,128)(2,1)} all-to-all(bf16[16,2,40,1024]{3,2,1,0:T(8,128)(2,1)S(1)} %get-tuple-element.8), channel_id=1, replica_groups=mesh['dp'=2,'expert'=16] {'expert'}, dimensions={0} | all-to-all | bytes 5242880 | tf_op jit(solution)/shard_map/all_to_all | solution.py:62
  117.6 9.7 %fusion.3 = bf16[16,2,40,1536]{3,2,0,1:T(8,128)(2,1)} fusion(bf16[2,1024,768]{2,1,0:T(8,128)(2,1)} %param.11, bf16[2,1024,768]{2,1,0:T(8,128)(2,1)} %param.10, bf16[16,2,40,1024]{3,2,1,0:T(8,128)(2,1)} %all_to_all.20), kind=kOutput, calls=%fused_computation.12 | convolution fusion | flops 4041080832 | bytes 12845056 | tf_op jit(solution)/shard_map/secd,edf->secf/dot_general | solution.py:68
  127.3 2.6 copy.33
  129.9 4.0 copy.36
  134.0 63.6 %all_to_all.21 = bf16[16,2,40,1024]{3,2,1,0:T(8,128)(2,1)S(1)} all-to-all(bf16[16,2,40,1024]{3,2,1,0:T(8,128)(2,1)} %get-tuple-element.7), channel_id=1, replica_groups=mesh['dp'=2,'expert'=16] {'expert'}, dimensions={0} | all-to-all | bytes 5242880 | tf_op jit(solution)/shard_map/all_to_all | solution.py:80
  197.6 3.6 convert_bitcast_fusion.2
  201.3 2.1 copy.37
  203.4 2.4 copy_convert_fusion
  205.8 55.2 %all-reduce.2.cloned.1.call-done = bf16[16,2,40,768]{3,2,0,1:T(8,128)(2,1)} async-done(((bf16[16,2,40,768]{3,2,0,1:T(8,128)(2,1)}), bf16[16,2,40,768]{3,2,0,1:T(8,128)(2,1)}) %all-reduce.2.cloned.1.call-update) | async-done | bytes 1966096 | tf_op jit(solution)/shard_map/psum | solution.py:82
  261.1 5.1 %fusion.16 = (bf16[8,2,40,768]{3,2,0,1:T(8,128)(2,1)}, bf16[8,2,40,768]{3,2,0,1:T(8,128)(2,1)}, bf16[8,2,40,768]{3,2,0,1:T(8,128)(2,1)}) fusion(f32[8,2,40,1536]{3,2,0,1:T(8,128)} %copy_convert_fusion, bf16[16,2,40,768]{3,2,0,1:T(8,128)(2,1)} %all-reduce.2.cloned.1.call-done, s32[]{:T(128)S(6)} %select_n.39), kind=kLoop, calls=%fused_computation.29 | loop fusion | flops 8355840 | bytes 7864324 | tf_op jit(solution)/shard_map/convert.2
  266.3 3.0 pad_maximum_fusion
  269.2 28.7 %all-gather.3.cloned.1.call-done = bf16[16,2,40,768]{3,2,0,1:T(8,128)(2,1)} async-done(((bf16[8,2,40,768]{3,2,0,1:T(8,128)(2,1)}), bf16[16,2,40,768]{3,2,0,1:T(8,128)(2,1)}) %all-gather.3.cloned.1.call-update) | async-done | bytes 1966096 | tf_op jit(solution)/shard_map/all_gather | solution.py:75
  298.0 3.8 convert_bitcast_fusion.1
  301.7 1.8 copy.28
  303.6 6.5 %all-to-all-start.1 = ((bf16[16,2,40,1024]{3,2,1,0:T(8,128)(2,1)}), bf16[16,2,40,1024]{3,2,1,0:T(8,128)(2,1)}, u32[]{:S(2)}, u32[]{:S(2)}) async-start(bf16[16,2,40,1024]{3,2,1,0:T(8,128)(2,1)} %copy.28), calls=%async_computation.1 | async-start | bytes 5242880 | tf_op jit(solution)/shard_map/all_to_all | solution.py:79
  310.1 43.1 %all-gather.5.cloned.1.call-done = bf16[16,2,40,1536]{3,2,0,1:T(8,128)(2,1)} async-done(((bf16[8,2,40,1536]{3,2,0,1:T(8,128)(2,1)}), bf16[16,2,40,1536]{3,2,0,1:T(8,128)(2,1)}) %all-gather.5.cloned.1.call-update) | async-done | bytes 3932176 | tf_op jit(solution)/shard_map/all_gather | solution.py:89
  353.2 8.3 %convert_bitcast_fusion = bf16[16,2,40,1024]{3,2,0,1:T(8,128)(2,1)S(1)} fusion(bf16[16,2,40,1536]{3,2,0,1:T(8,128)(2,1)} %all-gather.5.cloned.1.call-done, bf16[2,1024,768]{2,1,0:T(8,128)(2,1)} %param.11, bf16[2,1024,768]{2,1,0:T(8,128)(2,1)} %param.10), kind=kOutput, calls=%fused_computation.19 | convolution fusion | flops 4040425472 | bytes 12845056 | tf_op jit(solution)/shard_map/secf,edf->secd/dot_general | solution.py:90
  361.5 1.8 copy.30
  363.3 5.5 %all-to-all-done.1 = bf16[16,2,40,1024]{3,2,1,0:T(8,128)(2,1)} async-done(((bf16[16,2,40,1024]{3,2,1,0:T(8,128)(2,1)}), bf16[16,2,40,1024]{3,2,1,0:T(8,128)(2,1)}, u32[]{:S(2)}, u32[]{:S(2)}) %all-to-all-start.1) | async-done | bytes 2621472 | tf_op jit(solution)/shard_map/all_to_all | solution.py:79
  368.8 4.8 %all-to-all-start.3 = ((bf16[16,2,40,1024]{3,2,1,0:T(8,128)(2,1)}), bf16[16,2,40,1024]{3,2,1,0:T(8,128)(2,1)}, u32[]{:S(2)}, u32[]{:S(2)}) async-start(bf16[16,2,40,1024]{3,2,1,0:T(8,128)(2,1)} %copy.30), calls=%async_computation.3 | async-start | bytes 5242880 | tf_op jit(solution)/shard_map/all_to_all | solution.py:93
  373.7 8.1 %gather_fusion.1 = bf16[1024,1024]{1,0:T(8,128)(2,1)} fusion(bf16[1280,1024]{1,0:T(8,128)(2,1)} %bitcast.11, s32[1024]{0:T(1024)S(1)} %broadcast_clamp_fusion), kind=kCustom, calls=%fused_computation.1 | custom fusion | bytes 4198400 | tf_op jit(solution)/shard_map/gather | solution.py:45
  381.9 50.5 %all-to-all-done.3 = bf16[16,2,40,1024]{3,2,1,0:T(8,128)(2,1)} async-done(((bf16[16,2,40,1024]{3,2,1,0:T(8,128)(2,1)}), bf16[16,2,40,1024]{3,2,1,0:T(8,128)(2,1)}, u32[]{:S(2)}, u32[]{:S(2)}) %all-to-all-start.3) | async-done | bytes 2621472 | tf_op jit(solution)/shard_map/all_to_all | solution.py:93
  432.4 8.1 %gather_fusion.3 = bf16[1024,1024]{1,0:T(8,128)(2,1)} fusion(bf16[1280,1024]{1,0:T(8,128)(2,1)} %bitcast.18, s32[1024]{0:T(1024)S(1)} %broadcast_clamp_fusion), kind=kCustom, calls=%fused_computation.3 | custom fusion | bytes 4198400 | tf_op jit(solution)/shard_map/gather | solution.py:45
  440.5 6.7 %fusion = (bf16[128,1024]{1,0:T(8,128)(2,1)}, bf16[128,1024]{1,0:T(8,128)(2,1)}) fusion(bf16[1024,1024]{1,0:T(8,128)(2,1)} %gather_fusion.3, f32[128,8]{1,0:T(8,128)S(1)} %copy.21, bf16[1024,1024]{1,0:T(8,128)(2,1)} %gather_fusion.1), kind=kLoop, calls=%fused_computation.7 | loop fusion | flops 6029312 | bytes 4722688 | tf_op jit(solution)/shard_map/reduce_sum | solution.py:46
  (35 shorter events, 5.8 us)
Async XLA Ops:
  7.2 190.4 %copy-start = (bf16[2,768,1024]{2,1,0:T(8,128)(2,1)S(1)}, bf16[2,768,1024]{2,1,0:T(8,128)(2,1)}, u32[]{:S(2)}) copy-start(bf16[2,768,1024]{2,1,0:T(8,128)(2,1)} %param.12) | copy-start | bytes 9437188
  7.2 28.7 %copy-start.1 = (bf16[128,1024]{1,0:T(8,128)(2,1)S(1)}, bf16[128,1024]{1,0:T(8,128)(2,1)}, u32[]{:S(2)}) copy-start(bf16[128,1024]{1,0:T(8,128)(2,1)} %param.13) | copy-start | bytes 786436
  7.2 194.1 %reduce-scatter.5.cloned.1.call-start = ((), (), s32[]{:S(2)}) async-start(), calls=%async_computation.8 | async-start | bytes 5898240
  134.0 127.1 %all-reduce.2.cloned.1.call-start = ((), (), s32[]{:S(2)}) async-start(), calls=%async_computation.6 | async-start | bytes 3932160 | tf_op jit(solution)/shard_map/psum | solution.py:82
  201.2 96.7 %all-gather.3.cloned.1.call-start = ((), (), s32[]{:S(2)}) async-start(), calls=%async_computation.5 | async-start | bytes 2949120 | tf_op jit(solution)/shard_map/all_gather | solution.py:75
  266.2 87.0 %all-gather.5.cloned.1.call-start = ((), (), s32[]{:S(2)}) async-start(), calls=%async_computation.7 | async-start | bytes 5898240 | tf_op jit(solution)/shard_map/all_gather | solution.py:89
  303.6 65.3 %all-to-all-start.1 = ((bf16[16,2,40,1024]{3,2,1,0:T(8,128)(2,1)}), bf16[16,2,40,1024]{3,2,1,0:T(8,128)(2,1)}, u32[]{:S(2)}, u32[]{:S(2)}) async-start(bf16[16,2,40,1024]{3,2,1,0:T(8,128)(2,1)} %copy.28), calls=%async_computation.1 | async-start | bytes 5242880 | tf_op jit(solution)/shard_map/all_to_all | solution.py:79
  363.3 10.3 %copy-start.2 = (f32[128,8]{0,1:T(8,128)S(1)}, f32[128,8]{0,1:T(8,128)}, u32[]{:S(2)}) copy-start(f32[128,8]{0,1:T(8,128)} %param.9) | copy-start | bytes 12292
  368.8 63.5 %all-to-all-start.3 = ((bf16[16,2,40,1024]{3,2,1,0:T(8,128)(2,1)}), bf16[16,2,40,1024]{3,2,1,0:T(8,128)(2,1)}, u32[]{:S(2)}, u32[]{:S(2)}) async-start(bf16[16,2,40,1024]{3,2,1,0:T(8,128)(2,1)} %copy.30), calls=%async_computation.3 | async-start | bytes 5242880 | tf_op jit(solution)/shard_map/all_to_all | solution.py:93
Sparse Core Ops, SparseCore 0:
  134.1 51.6 reduce-scatter.4
  201.4 59.6 all-reduce.1
  266.3 31.6 all-gather.2
  299.4 53.7 all-gather.4
where the time goes:
time: 455 us; the launch traced here: 454 us
  waiting for transfers between devices  183 us (40%)
  blocking collectives  129 us (28%)
  local copies, waits for them, and re-layouts  51.8 us (11%)
  other arithmetic  39.5 us (9%)
  matrix products  25.4 us (6%)
  between operations  13.9 us (3%)
  starting transfers between devices  11.4 us (3%)
    all_to_all x1, blocking collectives, per_device(): lax.all_to_all(token_rows, 'expert', split_axis=0, concat_axis=0, tiled=T...  64.9 us
    all_to_all x1, blocking collectives, per_device(): lax.all_to_all(grad_rows_out, 'expert', split_axis=0, concat_axis=0, tile...  63.6 us
    psum x1, waiting for transfers between devices, per_device(): lax.psum(jnp.einsum('secd,efd->secf', piece, w_down, preferred_element_ty...  55.2 us
    all_to_all x1, waiting for transfers between devices, per_device(): lax.all_to_all(grad_rows, 'expert', split_axis=0, concat_axis=0, tiled=True)  50.5 us
    all_gather x1, waiting for transfers between devices, per_device(): lax.all_gather(act_grad(own_sums, own_back, hidden), 'dp', axis=0, tiled=...  43.1 us
    all_gather x1, waiting for transfers between devices, per_device(): lax.all_gather(activate(own_sums, hidden), 'dp', axis=0, tiled=True)  28.7 us
    another operation x4, other arithmetic  20.9 us
    gather x2, local copies, waits for them, and re-layouts, combine(): flat_rows[position].reshape(tok_rows, top_count, -1).astype(jnp.float32)  16.3 us
  transfers between devices with their start and end apart: 6, of which 5 were waited for; matrix products, arithmetic and copies ran while one was open for 8% of the time, Pallas kernels for 0%

commit v1 on v0

--- a/solution.py
+++ b/solution.py
@@ -2,6 +2,29 @@
 import jax.numpy as jnp
 from jax import lax
 from jax.sharding import PartitionSpec as P
+
+
+def split_up(x, dim, devices):
+    dims = x.shape
+    tiles = x.reshape(*dims[:dim], devices, dims[dim] // devices, *dims[dim + 1 :])
+    return jnp.moveaxis(tiles, dim, 0)
+
+
+def laid_out(blocks, dim):
+    dims = list(blocks.shape[1:])
+    dims[dim] *= blocks.shape[0]
+    return jnp.moveaxis(blocks, 0, dim).reshape(dims)
+
+
+def pairwise_exchange(x, axis, split_dim, concat_dim):
+    length, mine = (lax.axis_size(axis), lax.axis_index(axis))
+    blocks = split_up(x, split_dim, length)
+    outs = [blocks[mine]]
+    for step in range(1, length):
+        sent = blocks[mine ^ step]
+        outs.append(lax.ppermute(sent, axis, [(i, i ^ step) for i in range(length)]))
+    blocks = jnp.stack(outs)[mine ^ jnp.arange(length)]
+    return laid_out(blocks, concat_dim)
 
 
 def slot_table(expert_ids, experts, capacity):
@@ -77,7 +100,7 @@
         "secf,efd->secd", hidden_act, w_down, preferred_element_type=jnp.float32
     ).astype(jnp.bfloat16)
     out_returned = lax.all_to_all(expert_out, "expert", split_axis=0, concat_axis=0, tiled=True)
-    grad_recv = lax.all_to_all(grad_rows_out, "expert", split_axis=0, concat_axis=0, tiled=True)
+    grad_recv = pairwise_exchange(grad_rows_out, "expert", 0, 0)
     piece = grad_recv
     whole_back = lax.psum(
         jnp.einsum("secd,efd->secf", piece, w_down, preferred_element_type=jnp.float32).astype(

time: 455 us -> 467 us (1.026)
  blocking collectives: 129 us -> 64.9 us
  waiting for transfers between devices: 183 us -> 227 us
  starting transfers between devices: 11.4 us -> 27 us
  local copies, waits for them, and re-layouts: 51.8 us -> 64.8 us
    all_to_all x1 -> x0, blocking collectives: 63.6 us -> none  [per_device(): lax.all_to_all(grad_rows_out, 'expert', split_axis=0, concat_axis=0, tile...]
    ppermute x0 -> x15, waiting for transfers between devices: none -> 44.1 us  [pairwise_exchange(): lax.ppermute(sent, axis, [(i, i ^ step) for i in range(length)])]
    ppermute x0 -> x15, starting transfers between devices: none -> 15.4 us  [pairwise_exchange(): lax.ppermute(sent, axis, [(i, i ^ step) for i in range(length)])]
    unnamed x11 -> x27, local copies, waits for them, and re-layouts: 9.83 us -> 19.9 us
  transfers between devices with their start and end apart: 6 -> 21, of which waited for: 5 -> 15; matrix products, arithmetic and copies ran while one was open for 8% -> 13% of each run, Pallas kernels for 0% -> 0%
where the time goes in v1:
time: 467 us; the launch traced here: 465 us
  waiting for transfers between devices  227 us (49%)
  blocking collectives  64.9 us (14%)
  local copies, waits for them, and re-layouts  64.8 us (14%)
  other arithmetic  40.4 us (9%)
  matrix products  27.1 us (6%)
  starting transfers between devices  27 us (6%)
  between operations  14 us (3%)
    all_to_all x1, blocking collectives, per_device(): lax.all_to_all(token_rows, 'expert', split_axis=0, concat_axis=0, tiled=T...  64.9 us
    psum x1, waiting for transfers between devices, per_device(): lax.psum(jnp.einsum('secd,efd->secf', piece, w_down, preferred_element_ty...  54.9 us
    all_to_all x1, waiting for transfers between devices, per_device(): lax.all_to_all(grad_rows, 'expert', split_axis=0, concat_axis=0, tiled=True)  50.5 us
    ppermute x15, waiting for transfers between devices, pairwise_exchange(): lax.ppermute(sent, axis, [(i, i ^ step) for i in range(length)])  44.1 us
    all_gather x1, waiting for transfers between devices, per_device(): lax.all_gather(act_grad(own_sums, own_back, hidden), 'dp', axis=0, tiled=...  43.1 us
    all_gather x1, waiting for transfers between devices, per_device(): lax.all_gather(activate(own_sums, hidden), 'dp', axis=0, tiled=True)  28.7 us
    another operation x4, other arithmetic  20.9 us
    unnamed x27, local copies, waits for them, and re-layouts  19.9 us
  transfers between devices with their start and end apart: 21, of which 15 were waited for; matrix products, arithmetic and copies ran while one was open for 13% of the time, Pallas kernels for 0%

profile of v1, /device:TPU:11, one launch (start us, length us, event | category | flops | bytes accessed | tf_op | source)
XLA Modules:
  0.0 465.2 jit_solution(1795450855280467373)
XLA Ops:
  10.9 15.7 %reduce-window.6 = s32[32,8,128]{2,1,0:T(8,128)S(1)} reduce-window(s32[32,8,128]{2,1,0:T(8,128)} %fusion.23, s32[]{:T(128)} %constant.31.clone.1), window={size=1x1x128 pad=0_0x0_0x127_0}, to_apply=%region_0.0 | reduce-window | flops 4161536 | bytes 262148 | tf_op jit(solution)/shard_map/reduce-window
  31.5 4.3 scatter_custom_fusion
  36.0 5.1 %gather_fusion = bf16[1280,1024]{1,0:T(8,128)(2,1)} fusion(bf16[128,1024]{1,0:T(8,128)(2,1)S(1)} %copy-done.1, s32[2048]{0:T(1024)S(1)} %pad_clamp_fusion), kind=kCustom, calls=%fused_computation | custom fusion | bytes 5248000 | tf_op jit(solution)/shard_map/gather | solution.py:46
  43.1 64.9 %all_to_all.15 = bf16[16,2,40,1024]{3,2,1,0:T(8,128)(2,1)} all-to-all(bf16[16,2,40,1024]{3,2,1,0:T(8,128)(2,1)S(1)} %broadcast_select_fusion.1), channel_id=1, replica_groups=mesh['dp'=2,'expert'=16] {'expert'}, dimensions={0} | all-to-all | bytes 5242880 | tf_op jit(solution)/shard_map/all_to_all | solution.py:85
  108.0 9.7 %fusion.3 = bf16[16,2,40,1536]{3,2,0,1:T(8,128)(2,1)} fusion(bf16[2,1024,768]{2,1,0:T(8,128)(2,1)} %param.11, bf16[2,1024,768]{2,1,0:T(8,128)(2,1)} %param.10, bf16[16,2,40,1024]{3,2,1,0:T(8,128)(2,1)} %all_to_all.15), kind=kOutput, calls=%fused_computation.13 | convolution fusion | flops 4041080832 | bytes 12845056 | tf_op jit(solution)/shard_map/secd,edf->secf/dot_general | solution.py:91
  120.3 4.0 copy.37
  125.3 5.1 %gather_fusion.2 = bf16[1280,1024]{1,0:T(8,128)(2,1)} fusion(bf16[128,1024]{1,0:T(8,128)(2,1)S(1)} %copy-done.2, s32[2048]{0:T(1024)S(1)} %pad_clamp_fusion), kind=kCustom, calls=%fused_computation.2 | custom fusion | bytes 5248000 | tf_op jit(solution)/shard_map/gather | solution.py:46
  130.4 2.8 broadcast_select_fusion
  149.1 4.7 %collective-permute-done.5 = bf16[1,2,40,1024]{3,2,1,0:T(8,128)(2,1)S(1)} collective-permute-done((bf16[1,2,40,1024]{3,2,1,0:T(8,128)(2,1)S(1)}, bf16[1,2,40,1024]{3,2,1,0:T(8,128)(2,1)S(1)}, u32[]{:S(2)}, u32[]{:S(2)}) %collective-permute-start.5) | collective-permute-done | bytes 163872 | tf_op jit(solution)/shard_map/ppermute | solution.py:25
  153.8 4.9 %collective-permute-start.10 = (bf16[1,2,40,1024]{3,2,1,0:T(8,128)(2,1)S(1)}, bf16[1,2,40,1024]{3,2,1,0:T(8,128)(2,1)S(1)}, u32[]{:S(2)}, u32[]{:S(2)}) collective-permute-start(bf16[1,2,40,1024]{3,2,1,0:T(8,128)(2,1)S(1)} %get-tuple-element.11), channel_id=1, source_target_pairs={{0,11},{1,10},{2,9},{3,8},{4,15},{5,14},{6,13},{7,12},{8,3},{9,2},... | collective-permute-start | bytes 491528 | tf_op jit(solution)/shard_map/ppermute | solution.py:25
  162.1 11.6 %collective-permute-done.8 = bf16[1,2,40,1024]{3,2,1,0:T(8,128)(2,1)S(1)} collective-permute-done((bf16[1,2,40,1024]{3,2,1,0:T(8,128)(2,1)S(1)}, bf16[1,2,40,1024]{3,2,1,0:T(8,128)(2,1)S(1)}, u32[]{:S(2)}, u32[]{:S(2)}) %collective-permute-start.8) | collective-permute-done | bytes 163872 | tf_op jit(solution)/shard_map/ppermute | solution.py:25
  174.4 6.3 %collective-permute-done.9 = bf16[1,2,40,1024]{3,2,1,0:T(8,128)(2,1)S(1)} collective-permute-done((bf16[1,2,40,1024]{3,2,1,0:T(8,128)(2,1)S(1)}, bf16[1,2,40,1024]{3,2,1,0:T(8,128)(2,1)S(1)}, u32[]{:S(2)}, u32[]{:S(2)}) %collective-permute-start.9) | collective-permute-done | bytes 163872 | tf_op jit(solution)/shard_map/ppermute | solution.py:25
  181.4 4.7 %collective-permute-done.10 = bf16[1,2,40,1024]{3,2,1,0:T(8,128)(2,1)S(1)} collective-permute-done((bf16[1,2,40,1024]{3,2,1,0:T(8,128)(2,1)S(1)}, bf16[1,2,40,1024]{3,2,1,0:T(8,128)(2,1)S(1)}, u32[]{:S(2)}, u32[]{:S(2)}) %collective-permute-start.10) | collective-permute-done | bytes 163872 | tf_op jit(solution)/shard_map/ppermute | solution.py:25
  186.8 5.3 %collective-permute-done.11 = bf16[1,2,40,1024]{3,2,1,0:T(8,128)(2,1)S(1)} collective-permute-done((bf16[1,2,40,1024]{3,2,1,0:T(8,128)(2,1)S(1)}, bf16[1,2,40,1024]{3,2,1,0:T(8,128)(2,1)S(1)}, u32[]{:S(2)}, u32[]{:S(2)}) %collective-permute-start.11) | collective-permute-done | bytes 163872 | tf_op jit(solution)/shard_map/ppermute | solution.py:25
  196.1 3.5 collective-permute-done.13
  200.3 2.8 collective-permute-done.14
  203.8 4.0 gather_fusion.3
  207.8 5.3 %convert_bitcast_fusion.2 = bf16[16,2,40,768]{3,2,0,1:T(8,128)(2,1)} fusion(bf16[2,768,1024]{2,1,0:T(8,128)(2,1)S(1)} %copy-done, bf16[16,2,40,1024]{3,2,1,0:T(8,128)(2,1)} %gather_fusion.3), kind=kOutput, calls=%fused_computation.33 | convolution fusion | flops 2014248960 | bytes 7733248 | tf_op jit(solution)/shard_map/secd,efd->secf/dot_general | solution.py:106
  217.7 54.9 %all-reduce.2.cloned.1.call-done = bf16[16,2,40,768]{3,2,0,1:T(8,128)(2,1)} async-done(((bf16[16,2,40,768]{3,2,0,1:T(8,128)(2,1)}), bf16[16,2,40,768]{3,2,0,1:T(8,128)(2,1)}) %all-reduce.2.cloned.1.call-update) | async-done | bytes 1966096 | tf_op jit(solution)/shard_map/psum | solution.py:105
  272.6 5.1 %fusion.16 = (bf16[8,2,40,768]{3,2,0,1:T(8,128)(2,1)}, bf16[8,2,40,768]{3,2,0,1:T(8,128)(2,1)}, bf16[8,2,40,768]{3,2,0,1:T(8,128)(2,1)}) fusion(f32[8,2,40,1536]{3,2,0,1:T(8,128)} %copy_convert_fusion, bf16[16,2,40,768]{3,2,0,1:T(8,128)(2,1)} %all-reduce.2.cloned.1.call-done, s32[]{:T(128)S(6)} %select_n.120), kind=kLoop, calls=%fused_computation.30 | loop fusion | flops 8355840 | bytes 7864324 | tf_op jit(solution)/shard_map/convert.2
  277.8 3.0 pad_maximum_fusion
  280.8 28.7 %all-gather.3.cloned.1.call-done = bf16[16,2,40,768]{3,2,0,1:T(8,128)(2,1)} async-done(((bf16[8,2,40,768]{3,2,0,1:T(8,128)(2,1)}), bf16[16,2,40,768]{3,2,0,1:T(8,128)(2,1)}) %all-gather.3.cloned.1.call-update) | async-done | bytes 1966096 | tf_op jit(solution)/shard_map/all_gather | solution.py:98
  309.5 3.8 convert_bitcast_fusion.1
  315.1 6.5 %all-to-all-start.1 = ((bf16[16,2,40,1024]{3,2,1,0:T(8,128)(2,1)}), bf16[16,2,40,1024]{3,2,1,0:T(8,128)(2,1)}, u32[]{:S(2)}, u32[]{:S(2)}) async-start(bf16[16,2,40,1024]{3,2,1,0:T(8,128)(2,1)} %copy.29), calls=%async_computation.1 | async-start | bytes 5242880 | tf_op jit(solution)/shard_map/all_to_all | solution.py:102
  321.6 43.1 %all-gather.5.cloned.1.call-done = bf16[16,2,40,1536]{3,2,0,1:T(8,128)(2,1)} async-done(((bf16[8,2,40,1536]{3,2,0,1:T(8,128)(2,1)}), bf16[16,2,40,1536]{3,2,0,1:T(8,128)(2,1)}) %all-gather.5.cloned.1.call-update) | async-done | bytes 3932176 | tf_op jit(solution)/shard_map/all_gather | solution.py:112
  364.7 8.3 %convert_bitcast_fusion = bf16[16,2,40,1024]{3,2,0,1:T(8,128)(2,1)S(1)} fusion(bf16[16,2,40,1536]{3,2,0,1:T(8,128)(2,1)} %all-gather.5.cloned.1.call-done, bf16[2,1024,768]{2,1,0:T(8,128)(2,1)} %param.11, bf16[2,1024,768]{2,1,0:T(8,128)(2,1)} %param.10), kind=kOutput, calls=%fused_computation.20 | convolution fusion | flops 4040425472 | bytes 12845056 | tf_op jit(solution)/shard_map/secf,edf->secd/dot_general | solution.py:113
  374.8 5.5 %all-to-all-done.1 = bf16[16,2,40,1024]{3,2,1,0:T(8,128)(2,1)} async-done(((bf16[16,2,40,1024]{3,2,1,0:T(8,128)(2,1)}), bf16[16,2,40,1024]{3,2,1,0:T(8,128)(2,1)}, u32[]{:S(2)}, u32[]{:S(2)}) %all-to-all-start.1) | async-done | bytes 2621472 | tf_op jit(solution)/shard_map/all_to_all | solution.py:102
  380.4 4.8 %all-to-all-start.2 = ((bf16[16,2,40,1024]{3,2,1,0:T(8,128)(2,1)}), bf16[16,2,40,1024]{3,2,1,0:T(8,128)(2,1)}, u32[]{:S(2)}, u32[]{:S(2)}) async-start(bf16[16,2,40,1024]{3,2,1,0:T(8,128)(2,1)} %copy.31), calls=%async_computation.2 | async-start | bytes 5242880 | tf_op jit(solution)/shard_map/all_to_all | solution.py:116
  385.3 8.1 %gather_fusion.1 = bf16[1024,1024]{1,0:T(8,128)(2,1)} fusion(bf16[1280,1024]{1,0:T(8,128)(2,1)} %bitcast.11, s32[1024]{0:T(1024)S(1)} %broadcast_clamp_fusion), kind=kCustom, calls=%fused_computation.1 | custom fusion | bytes 4198400 | tf_op jit(solution)/shard_map/gather | solution.py:68
  393.4 50.5 %all-to-all-done.2 = bf16[16,2,40,1024]{3,2,1,0:T(8,128)(2,1)} async-done(((bf16[16,2,40,1024]{3,2,1,0:T(8,128)(2,1)}), bf16[16,2,40,1024]{3,2,1,0:T(8,128)(2,1)}, u32[]{:S(2)}, u32[]{:S(2)}) %all-to-all-start.2) | async-done | bytes 2621472 | tf_op jit(solution)/shard_map/all_to_all | solution.py:116
  443.9 8.1 %gather_fusion.4 = bf16[1024,1024]{1,0:T(8,128)(2,1)} fusion(bf16[1280,1024]{1,0:T(8,128)(2,1)} %bitcast.50, s32[1024]{0:T(1024)S(1)} %broadcast_clamp_fusion), kind=kCustom, calls=%fused_computation.4 | custom fusion | bytes 4198400 | tf_op jit(solution)/shard_map/gather | solution.py:68
  452.0 6.7 %fusion = (bf16[128,1024]{1,0:T(8,128)(2,1)}, bf16[128,1024]{1,0:T(8,128)(2,1)}) fusion(bf16[1024,1024]{1,0:T(8,128)(2,1)} %gather_fusion.4, f32[128,8]{1,0:T(8,128)S(1)} %copy.22, bf16[1024,1024]{1,0:T(8,128)(2,1)} %gather_fusion.1), kind=kLoop, calls=%fused_computation.8 | loop fusion | flops 6029312 | bytes 4722688 | tf_op jit(solution)/shard_map/reduce_sum | solution.py:69
  (86 shorter events, 49.4 us)
Async XLA Ops:
  7.2 200.6 %copy-start = (bf16[2,768,1024]{2,1,0:T(8,128)(2,1)S(1)}, bf16[2,768,1024]{2,1,0:T(8,128)(2,1)}, u32[]{:S(2)}) copy-start(bf16[2,768,1024]{2,1,0:T(8,128)(2,1)} %param.12) | copy-start | bytes 9437188
  7.2 28.8 %copy-start.1 = (bf16[128,1024]{1,0:T(8,128)(2,1)S(1)}, bf16[128,1024]{1,0:T(8,128)(2,1)}, u32[]{:S(2)}) copy-start(bf16[128,1024]{1,0:T(8,128)(2,1)} %param.7) | copy-start | bytes 786436
  7.2 206.0 %reduce-scatter.5.cloned.1.call-start = ((), (), s32[]{:S(2)}) async-start(), calls=%async_computation.7 | async-start | bytes 5898240
  124.3 0.9 copy-start.2
  124.4 148.2 %all-reduce.2.cloned.1.call-start = ((), (), s32[]{:S(2)}) async-start(), calls=%async_computation.5 | async-start | bytes 3932160 | tf_op jit(solution)/shard_map/psum | solution.py:105
  134.1 3.7 collective-permute-start
  134.2 5.5 %collective-permute-start.1 = (bf16[1,2,40,1024]{3,2,1,0:T(8,128)(2,1)S(1)}, bf16[1,2,40,1024]{3,2,1,0:T(8,128)(2,1)S(1)}, u32[]{:S(2)}, u32[]{:S(2)}) collective-permute-start(bf16[1,2,40,1024]{3,2,1,0:T(8,128)(2,1)S(1)} %get-tuple-element.20), channel_id=1, source_target_pairs={{0,2},{1,3},{2,0},{3,1},{4,6},{5,7},{6,4},{7,5},{8,10},{9,11},{10,... | collective-permute-start | bytes 491528 | tf_op jit(solution)/shard_map/ppermute | solution.py:25
  134.7 9.3 %collective-permute-start.2 = (bf16[1,2,40,1024]{3,2,1,0:T(8,128)(2,1)S(1)}, bf16[1,2,40,1024]{3,2,1,0:T(8,128)(2,1)S(1)}, u32[]{:S(2)}, u32[]{:S(2)}) collective-permute-start(bf16[1,2,40,1024]{3,2,1,0:T(8,128)(2,1)S(1)} %get-tuple-element.19), channel_id=1, source_target_pairs={{0,3},{1,2},{2,1},{3,0},{4,7},{5,6},{6,5},{7,4},{8,11},{9,10},{10,... | collective-permute-start | bytes 491528 | tf_op jit(solution)/shard_map/ppermute | solution.py:25
  136.2 9.6 %collective-permute-start.3 = (bf16[1,2,40,1024]{3,2,1,0:T(8,128)(2,1)S(1)}, bf16[1,2,40,1024]{3,2,1,0:T(8,128)(2,1)S(1)}, u32[]{:S(2)}, u32[]{:S(2)}) collective-permute-start(bf16[1,2,40,1024]{3,2,1,0:T(8,128)(2,1)S(1)} %get-tuple-element.18), channel_id=1, source_target_pairs={{0,4},{1,5},{2,6},{3,7},{4,0},{5,1},{6,2},{7,3},{8,12},{9,13},{10,... | collective-permute-start | bytes 491528 | tf_op jit(solution)/shard_map/ppermute | solution.py:25
  136.6 10.9 %collective-permute-start.4 = (bf16[1,2,40,1024]{3,2,1,0:T(8,128)(2,1)S(1)}, bf16[1,2,40,1024]{3,2,1,0:T(8,128)(2,1)S(1)}, u32[]{:S(2)}, u32[]{:S(2)}) collective-permute-start(bf16[1,2,40,1024]{3,2,1,0:T(8,128)(2,1)S(1)} %get-tuple-element.17), channel_id=1, source_target_pairs={{0,5},{1,4},{2,7},{3,6},{4,1},{5,0},{6,3},{7,2},{8,13},{9,12},{10,... | collective-permute-start | bytes 491528 | tf_op jit(solution)/shard_map/ppermute | solution.py:25
  137.8 16.0 %collective-permute-start.5 = (bf16[1,2,40,1024]{3,2,1,0:T(8,128)(2,1)S(1)}, bf16[1,2,40,1024]{3,2,1,0:T(8,128)(2,1)S(1)}, u32[]{:S(2)}, u32[]{:S(2)}) collective-permute-start(bf16[1,2,40,1024]{3,2,1,0:T(8,128)(2,1)S(1)} %get-tuple-element.16), channel_id=1, source_target_pairs={{0,6},{1,7},{2,4},{3,5},{4,2},{5,3},{6,0},{7,1},{8,14},{9,15},{10,... | collective-permute-start | bytes 491528 | tf_op jit(solution)/shard_map/ppermute | solution.py:25
  139.7 19.6 %collective-permute-start.6 = (bf16[1,2,40,1024]{3,2,1,0:T(8,128)(2,1)S(1)}, bf16[1,2,40,1024]{3,2,1,0:T(8,128)(2,1)S(1)}, u32[]{:S(2)}, u32[]{:S(2)}) collective-permute-start(bf16[1,2,40,1024]{3,2,1,0:T(8,128)(2,1)S(1)} %get-tuple-element.15), channel_id=1, source_target_pairs={{0,7},{1,6},{2,5},{3,4},{4,3},{5,2},{6,1},{7,0},{8,15},{9,14},{10,... | collective-permute-start | bytes 491528 | tf_op jit(solution)/shard_map/ppermute | solution.py:25
  144.1 16.0 %collective-permute-start.7 = (bf16[1,2,40,1024]{3,2,1,0:T(8,128)(2,1)S(1)}, bf16[1,2,40,1024]{3,2,1,0:T(8,128)(2,1)S(1)}, u32[]{:S(2)}, u32[]{:S(2)}) collective-permute-start(bf16[1,2,40,1024]{3,2,1,0:T(8,128)(2,1)S(1)} %get-tuple-element.14), channel_id=1, source_target_pairs={{0,8},{1,9},{2,10},{3,11},{4,12},{5,13},{6,14},{7,15},{8,0},{9,1},... | collective-permute-start | bytes 491528 | tf_op jit(solution)/shard_map/ppermute | solution.py:25
  145.9 27.8 %collective-permute-start.8 = (bf16[1,2,40,1024]{3,2,1,0:T(8,128)(2,1)S(1)}, bf16[1,2,40,1024]{3,2,1,0:T(8,128)(2,1)S(1)}, u32[]{:S(2)}, u32[]{:S(2)}) collective-permute-start(bf16[1,2,40,1024]{3,2,1,0:T(8,128)(2,1)S(1)} %get-tuple-element.13), channel_id=1, source_target_pairs={{0,9},{1,8},{2,11},{3,10},{4,13},{5,12},{6,15},{7,14},{8,1},{9,0},... | collective-permute-start | bytes 491528 | tf_op jit(solution)/shard_map/ppermute | solution.py:25
  147.4 33.3 %collective-permute-start.9 = (bf16[1,2,40,1024]{3,2,1,0:T(8,128)(2,1)S(1)}, bf16[1,2,40,1024]{3,2,1,0:T(8,128)(2,1)S(1)}, u32[]{:S(2)}, u32[]{:S(2)}) collective-permute-start(bf16[1,2,40,1024]{3,2,1,0:T(8,128)(2,1)S(1)} %get-tuple-element.12), channel_id=1, source_target_pairs={{0,10},{1,11},{2,8},{3,9},{4,14},{5,15},{6,12},{7,13},{8,2},{9,3},... | collective-permute-start | bytes 491528 | tf_op jit(solution)/shard_map/ppermute | solution.py:25
  153.8 32.3 %collective-permute-start.10 = (bf16[1,2,40,1024]{3,2,1,0:T(8,128)(2,1)S(1)}, bf16[1,2,40,1024]{3,2,1,0:T(8,128)(2,1)S(1)}, u32[]{:S(2)}, u32[]{:S(2)}) collective-permute-start(bf16[1,2,40,1024]{3,2,1,0:T(8,128)(2,1)S(1)} %get-tuple-element.11), channel_id=1, source_target_pairs={{0,11},{1,10},{2,9},{3,8},{4,15},{5,14},{6,13},{7,12},{8,3},{9,2},... | collective-permute-start | bytes 491528 | tf_op jit(solution)/shard_map/ppermute | solution.py:25
  159.3 32.7 %collective-permute-start.11 = (bf16[1,2,40,1024]{3,2,1,0:T(8,128)(2,1)S(1)}, bf16[1,2,40,1024]{3,2,1,0:T(8,128)(2,1)S(1)}, u32[]{:S(2)}, u32[]{:S(2)}) collective-permute-start(bf16[1,2,40,1024]{3,2,1,0:T(8,128)(2,1)S(1)} %get-tuple-element.10), channel_id=1, source_target_pairs={{0,12},{1,13},{2,14},{3,15},{4,8},{5,9},{6,10},{7,11},{8,4},{9,5},... | collective-permute-start | bytes 491528 | tf_op jit(solution)/shard_map/ppermute | solution.py:25
  160.1 35.4 %collective-permute-start.12 = (bf16[1,2,40,1024]{3,2,1,0:T(8,128)(2,1)S(1)}, bf16[1,2,40,1024]{3,2,1,0:T(8,128)(2,1)S(1)}, u32[]{:S(2)}, u32[]{:S(2)}) collective-permute-start(bf16[1,2,40,1024]{3,2,1,0:T(8,128)(2,1)S(1)} %get-tuple-element.9), channel_id=1, source_target_pairs={{0,13},{1,12},{2,15},{3,14},{4,9},{5,8},{6,11},{7,10},{8,5},{9,4},... | collective-permute-start | bytes 491528 | tf_op jit(solution)/shard_map/ppermute | solution.py:25
  173.7 25.9 %collective-permute-start.13 = (bf16[1,2,40,1024]{3,2,1,0:T(8,128)(2,1)S(1)}, bf16[1,2,40,1024]{3,2,1,0:T(8,128)(2,1)S(1)}, u32[]{:S(2)}, u32[]{:S(2)}) collective-permute-start(bf16[1,2,40,1024]{3,2,1,0:T(8,128)(2,1)S(1)} %get-tuple-element.8), channel_id=1, source_target_pairs={{0,14},{1,15},{2,12},{3,13},{4,10},{5,11},{6,8},{7,9},{8,6},{9,7},... | collective-permute-start | bytes 491528 | tf_op jit(solution)/shard_map/ppermute | solution.py:25
  180.7 22.4 %collective-permute-start.14 = (bf16[1,2,40,1024]{3,2,1,0:T(8,128)(2,1)S(1)}, bf16[1,2,40,1024]{3,2,1,0:T(8,128)(2,1)S(1)}, u32[]{:S(2)}, u32[]{:S(2)}) collective-permute-start(bf16[1,2,40,1024]{3,2,1,0:T(8,128)(2,1)S(1)} %get-tuple-element.7), channel_id=1, source_target_pairs={{0,15},{1,14},{2,13},{3,12},{4,11},{5,10},{6,9},{7,8},{8,7},{9,6},... | collective-permute-start | bytes 491528 | tf_op jit(solution)/shard_map/ppermute | solution.py:25
  213.1 96.4 %all-gather.3.cloned.1.call-start = ((), (), s32[]{:S(2)}) async-start(), calls=%async_computation.4 | async-start | bytes 2949120 | tf_op jit(solution)/shard_map/all_gather | solution.py:98
  277.7 87.0 %all-gather.5.cloned.1.call-start = ((), (), s32[]{:S(2)}) async-start(), calls=%async_computation.6 | async-start | bytes 5898240 | tf_op jit(solution)/shard_map/all_gather | solution.py:112
  315.1 65.3 %all-to-all-start.1 = ((bf16[16,2,40,1024]{3,2,1,0:T(8,128)(2,1)}), bf16[16,2,40,1024]{3,2,1,0:T(8,128)(2,1)}, u32[]{:S(2)}, u32[]{:S(2)}) async-start(bf16[16,2,40,1024]{3,2,1,0:T(8,128)(2,1)} %copy.29), calls=%async_computation.1 | async-start | bytes 5242880 | tf_op jit(solution)/shard_map/all_to_all | solution.py:102
  374.8 10.3 %copy-start.3 = (f32[128,8]{0,1:T(8,128)S(1)}, f32[128,8]{0,1:T(8,128)}, u32[]{:S(2)}) copy-start(f32[128,8]{0,1:T(8,128)} %param.9) | copy-start | bytes 12292
  380.4 63.5 %all-to-all-start.2 = ((bf16[16,2,40,1024]{3,2,1,0:T(8,128)(2,1)}), bf16[16,2,40,1024]{3,2,1,0:T(8,128)(2,1)}, u32[]{:S(2)}, u32[]{:S(2)}) async-start(bf16[16,2,40,1024]{3,2,1,0:T(8,128)(2,1)} %copy.31), calls=%async_computation.2 | async-start | bytes 5242880 | tf_op jit(solution)/shard_map/all_to_all | solution.py:116
Sparse Core Ops, SparseCore 0:
  124.5 51.6 reduce-scatter.4
  213.2 59.3 all-reduce.1
  277.9 31.6 all-gather.2
  310.9 53.7 all-gather.4
